TPU v7x, 32 devices: a whole 2x2x4 slice. The times are simulated.
32 devices in a mesh: row: 8 (over y, x, core), ck: 4 (over z).
Axes of the slice: x: 2, y: 2, z: 4, core: 2. Of those that a mesh axis runs over, the one named last changes fastest.
Arguments:
- amp_tiles: bfloat16 [8, 4, 8, 16, 128, 128], P('row', 'ck'), may hold values from -6 to 6
- tile_pos: int32 [8, 4, 8, 16], P(None, 'ck'), may hold values from 0 to 2303, as said below
- tile_count: int32 [8, 4, 8], P(None, 'ck'), may hold values from 0 to 16, as said below
- cycle_integrals: bfloat16 [147456, 512], P('ck'), may hold values from -0.09375 to 0.09375
- row_gap: float32 [8192], P(('row', 'ck')), may hold values from 0.5 to 4
- col_gap: float32 [512], replicated, may hold values from 0.5 to 4
Outputs:
- new_amp: bfloat16 [8192, 512], P(('row', 'ck'))
Inputs may be any that keep to these rules, and one draw needn't show every extreme that they name: `tile_pos`: slots 0 to tile_count - 1 of each list are live, the others hold no tile. Within one ck group and one row owner all slots' positions are distinct. `tile_count`: in every ck group one row owner receives 16 live tiles from every storage owner.
All inputs are finite; a program needn't handle non-finite values.
Results may differ from a plain program's by a relative error of at most 0.001.
Values may be sent and summed in bfloat16 or wider, within the bound.
No kernel may reach another device: no remote copies, remote signals or barrier semaphores. Data moves between devices by JAX's collectives and lax.ppermute only.
A program may use at most 320 MiB of HBM per device.

v0:
```python
import jax
import jax.numpy as jnp
from jax import lax
from jax.sharding import PartitionSpec as P

TILE = 128
KT_DEV = 288
CAP = 16


def slot_products(amp_slots, positions, integrals):
    tile_width = amp_slots.shape[-1]
    blocks = integrals.reshape(-1, tile_width, integrals.shape[-1])
    picked = blocks[positions % blocks.shape[0]]
    return jnp.einsum("mrk,mkc->mrc", amp_slots, picked, preferred_element_type=jnp.float32)


def row_terms(products, tile_ids, live_mask, row_count):
    tile_width = products.shape[1]
    segment_total = row_count // tile_width
    inside = live_mask & (tile_ids >= 0) & (tile_ids < segment_total)
    target = jnp.where(inside, tile_ids, segment_total)
    summed = jax.ops.segment_sum(products, target, num_segments=segment_total + 1)[:segment_total]
    return summed.reshape(row_count, products.shape[2])


def on_device(amp_tiles, tile_pos, tile_count, cycle_integrals, row_gap, col_gap):
    my_row = lax.axis_index("row")
    slot_range = jnp.arange(CAP)
    share_rows = row_gap.shape[0]
    received = lax.all_to_all(amp_tiles, "row", split_axis=2, concat_axis=0, tiled=True)
    amp_slots = received.reshape(-1, TILE, TILE)
    positions = lax.dynamic_index_in_dim(tile_pos, my_row, 2, keepdims=False).reshape(-1)
    counts = lax.dynamic_index_in_dim(tile_count, my_row, 2, keepdims=False).reshape(-1)
    live_mask = (slot_range[None, :] < counts[:, None]).reshape(-1)
    tile_ids = positions // KT_DEV
    products = slot_products(amp_slots, positions, cycle_integrals)
    reduced = lax.psum_scatter(
        row_terms(products, tile_ids, live_mask, lax.axis_size("ck") * share_rows),
        "ck",
        scatter_dimension=0,
        tiled=True,
    )
    quotient = (reduced / (row_gap[:, None] + col_gap[None, :])).astype(jnp.bfloat16)
    return lax.all_to_all(quotient, "row", split_axis=0, concat_axis=0, tiled=True)


def solution(mesh):
    return jax.shard_map(
        on_device,
        mesh=mesh,
        in_specs=(
            P("row", "ck", None, None, None, None),
            P(None, "ck", None, None),
            P(None, "ck", None),
            P("ck", None),
            P(("row", "ck")),
            P(),
        ),
        out_specs=P(("row", "ck"), None),
        check_vma=False,
    )
```

profile of v0, /device:TPU:0, one launch (start us, length us, event | category | flops | bytes accessed | tf_op | source)
XLA Modules:
  0.0 227.3 jit_solution(11846260106764262696)
XLA Ops:
  6.5 0.0 copy-start
  6.5 5.3 %all-to-all-start = ((bf16[1,1,8,16,128,128]{5,4,3,1,0,2:T(8,128)(2,1)}), bf16[1,1,8,16,128,128]{5,4,3,1,0,2:T(8,128)(2,1)}, u32[]{:S(2)}, u32[]{:S(2)}) async-start(bf16[1,1,8,16,128,128]{5,4,3,1,0,2:T(8,128)(2,1)} %bitcast.16), calls=%async_computation | async-start | bytes 8388608 | tf_op jit(solution)/shard_map/all_to_all | solution.py:31
  11.9 0.0 reduce-scatter.2.cloned.1.call-start
  11.9 0.8 remainder_reduce_fusion
  12.7 0.1 div.20
  12.8 0.1 rem.30
  12.9 0.0 copy-done
  12.9 0.3 dynamic-slice_reduce_fusion
  13.2 0.1 iota_compare_fusion
  13.3 0.1 lt.66
  13.4 0.8 compare_reduce_fusion
  14.2 0.1 ne.52
  14.3 12.6 %gather_fusion = bf16[128,128,512]{2,1,0:T(8,128)(2,1)} fusion(bf16[288,128,512]{2,1,0:T(8,128)(2,1)} %bitcast.15, s32[1024]{0:T(1024)S(1)} %pad_clamp_fusion), kind=kCustom, calls=%fused_computation | custom fusion | bytes 33554944 | tf_op jit(solution)/shard_map/gather | solution.py:14
  26.9 34.2 %all-to-all-done = bf16[1,1,8,16,128,128]{5,4,3,1,0,2:T(8,128)(2,1)} async-done(((bf16[1,1,8,16,128,128]{5,4,3,1,0,2:T(8,128)(2,1)}), bf16[1,1,8,16,128,128]{5,4,3,1,0,2:T(8,128)(2,1)}, u32[]{:S(2)}, u32[]{:S(2)}) %all-to-all-start) | async-done | bytes 4194336 | tf_op jit(solution)/shard_map/all_to_all | solution.py:31
  61.1 22.3 %convolution_bitcast_fusion = f32[128,128,512]{1,2,0:T(8,128)} fusion(bf16[128,128,512]{2,1,0:T(8,128)(2,1)} %gather_fusion, bf16[128,128,128]{2,1,0:T(8,128)(2,1)} %bitcast.4), kind=kOutput, calls=%fused_computation.2 | convolution fusion | flops 2147483648 | bytes 54525952 | tf_op jit(solution)/shard_map/mrk,mkc->mrc/dot_general | solution.py:15
  83.4 33.4 %copy.12 = f32[128,128,512]{2,1,0:T(8,128)} copy(f32[128,128,512]{1,2,0:T(8,128)} %convolution_bitcast_fusion) | data formatting | bytes 67108864 | tf_op jit(solution)/shard_map/mrk,mkc->mrc/dot_general | solution.py:15
  116.8 0.3 broadcast_in_dim.3
  117.1 0.0 copy-start.2
  117.1 0.0 copy-start.3
  117.1 0.0 copy-start.1
  117.2 45.1 %scatter_fusion = f32[9,128,512]{2,1,0:T(8,128)S(1)} fusion(f32[9,128,512]{2,1,0:T(8,128)S(1)} %broadcast_in_dim.3, s32[128]{0:T(128)S(1)} %get-tuple-element.8, f32[128,128,512]{2,1,0:T(8,128)} %copy.12), kind=kCustom, calls=%fused_computation.1 | custom fusion | flops 8388608 | bytes 100663808 | tf_op jit(solution)/shard_map/scatter-add | solution.py:23
  162.3 1.6 slice.6
  163.9 0.0 reduce-scatter.2.cloned.1.call-update
  163.9 44.3 %reduce-scatter.2.cloned.1.call-done = f32[256,512]{1,0:T(8,128)} async-done(((f32[1024,512]{1,0:T(8,128)}), f32[256,512]{1,0:T(8,128)}) %reduce-scatter.2.cloned.1.call-update) | async-done | bytes 524304 | tf_op jit(solution)/shard_map/reduce_scatter | solution.py:38
  208.2 0.0 copy-done.2
  208.2 0.0 copy-done.3
  208.2 1.2 divide_convert_fusion
  209.4 10.4 %all_to_all.21 = bf16[8,32,512]{2,1,0:T(8,128)(2,1)S(1)} all-to-all(bf16[8,32,512]{2,1,0:T(8,128)(2,1)S(1)} %bitcast.17), channel_id=1, replica_groups=mesh['row'=8,'ck'=4] {'row'}, dimensions={0} | all-to-all | bytes 524288 | tf_op jit(solution)/shard_map/all_to_all | solution.py:45
  219.7 0.7 copy.16
  220.4 0.0 copy-done.1
  (2 shorter events, 0.0 us)
Async XLA Ops:
  6.5 6.4 %copy-start = (s32[8,1,8]{2,1,0:T(1,128)S(1)}, s32[8,1,8]{2,1,0:T(1,128)}, u32[]{:S(2)}) copy-start(s32[8,1,8]{2,1,0:T(1,128)} %param.8) | copy-start | bytes 772
  6.5 54.5 %all-to-all-start = ((bf16[1,1,8,16,128,128]{5,4,3,1,0,2:T(8,128)(2,1)}), bf16[1,1,8,16,128,128]{5,4,3,1,0,2:T(8,128)(2,1)}, u32[]{:S(2)}, u32[]{:S(2)}) async-start(bf16[1,1,8,16,128,128]{5,4,3,1,0,2:T(8,128)(2,1)} %bitcast.16), calls=%async_computation | async-start | bytes 8388608 | tf_op jit(solution)/shard_map/all_to_all | solution.py:31
  11.9 196.3 %reduce-scatter.2.cloned.1.call-start = ((), (), s32[]{:S(2)}) async-start(), calls=%async_computation.3 | async-start | bytes 2621440 | tf_op jit(solution)/shard_map/reduce_scatter | solution.py:38
  117.1 91.1 %copy-start.2 = (f32[512]{0:T(512)S(1)}, f32[512]{0:T(512)}, u32[]{:S(2)}) copy-start(f32[512]{0:T(512)} %param.11) | copy-start | bytes 6148
  117.1 91.1 %copy-start.3 = (f32[256]{0:T(256)S(1)}, f32[256]{0:T(256)}, u32[]{:S(2)}) copy-start(f32[256]{0:T(256)} %param.10) | copy-start | bytes 3076
  117.1 103.3 %copy-start.1 = (s32[8,1,8]{2,1,0:T(1,128)S(1)}, s32[8,1,8]{2,1,0:T(1,128)}, u32[]{:S(2)}) copy-start(s32[8,1,8]{2,1,0:T(1,128)} %param.8) | copy-start | bytes 772
Sparse Core Ops, SparseCore 0:
  164.0 44.0 reduce-scatter.1
where the time goes:
time: 229 us; the launch traced here: 227 us
  waiting for transfers between devices  78.5 us (34%)
  local copies, waits for them, and re-layouts  49.3 us (22%)
  other arithmetic  48 us (21%)
  matrix products  22.3 us (10%)
  between operations  13.5 us (6%)
  blocking collectives  10.4 us (5%)
  starting transfers between devices  5.37 us (2%)
    scatter-add x1, other arithmetic, row_terms(): jax.ops.segment_sum(products, target, num_segments=segment_total + 1)  45.1 us
    reduce_scatter x1, waiting for transfers between devices, on_device(): lax.psum_scatter(row_terms(products, tile_ids, live_mask, lax.axis_size('...  44.3 us
    all_to_all x1, waiting for transfers between devices, on_device(): lax.all_to_all(amp_tiles, 'row', split_axis=2, concat_axis=0, tiled=True)  34.2 us
    dot_general x1, local copies, waits for them, and re-layouts, slot_products(): jnp.einsum('mrk,mkc->mrc', amp_slots, picked, preferred_element_type=jnp....  33.4 us
    dot_general x1, matrix products, slot_products(): jnp.einsum('mrk,mkc->mrc', amp_slots, picked, preferred_element_type=jnp....  22.3 us
    gather x1, local copies, waits for them, and re-layouts, slot_products(): picked = blocks[positions % blocks.shape[0]]  12.6 us
    all_to_all x1, blocking collectives, on_device(): lax.all_to_all(quotient, 'row', split_axis=0, concat_axis=0, tiled=True)  10.4 us
    all_to_all x1, starting transfers between devices, on_device(): lax.all_to_all(amp_tiles, 'row', split_axis=2, concat_axis=0, tiled=True)  5.33 us
  transfers between devices with their start and end apart: 2, of which 2 were waited for; matrix products, arithmetic and copies ran while one was open for 7% of the time, Pallas kernels for 0%

commit v1 on v0

--- a/solution.py
+++ b/solution.py
@@ -6,6 +6,17 @@
 TILE = 128
 KT_DEV = 288
 CAP = 16
+
+
+def in_blocks(value, dim, size):
+    before, after = (value.shape[:dim], value.shape[dim + 1 :])
+    return jnp.moveaxis(value.reshape(*before, size, -1, *after), dim, 0)
+
+
+def laid_out(pieces, dim):
+    dims = list(pieces.shape[1:])
+    dims[dim] *= pieces.shape[0]
+    return jnp.moveaxis(pieces, 0, dim).reshape(dims)
 
 
 def slot_products(amp_slots, positions, integrals):
@@ -28,7 +39,14 @@
     my_row = lax.axis_index("row")
     slot_range = jnp.arange(CAP)
     share_rows = row_gap.shape[0]
-    received = lax.all_to_all(amp_tiles, "row", split_axis=2, concat_axis=0, tiled=True)
+    size, here = (lax.axis_size("row"), lax.axis_index("row"))
+    blocks_2 = in_blocks(amp_tiles, 2, size)
+    finished = [blocks_2[here]]
+    for turn in range(1, size):
+        sent = blocks_2[here ^ turn]
+        finished.append(lax.ppermute(sent, "row", [(i, i ^ turn) for i in range(size)]))
+    blocks_2 = jnp.stack(finished)[here ^ jnp.arange(size)]
+    received = laid_out(blocks_2, 0)
     amp_slots = received.reshape(-1, TILE, TILE)
     positions = lax.dynamic_index_in_dim(tile_pos, my_row, 2, keepdims=False).reshape(-1)
     counts = lax.dynamic_index_in_dim(tile_count, my_row, 2, keepdims=False).reshape(-1)

time: 229 us -> 200 us (0.87)
  waiting for transfers between devices: 78.5 us -> 63.5 us
  local copies, waits for them, and re-layouts: 49.3 us -> 37.4 us
  matrix products: 22.3 us -> 17.9 us
  starting transfers between devices: 5.37 us -> 7.93 us
    all_to_all x1 -> x0, waiting for transfers between devices: 34.2 us -> none  [on_device(): lax.all_to_all(amp_tiles, 'row', split_axis=2, concat_axis=0, tiled=True)]
    dot_general x1 -> x0, local copies, waits for them, and re-layouts: 33.4 us -> none  [slot_products(): jnp.einsum('mrk,mkc->mrc', amp_slots, picked, preferred_element_type=jnp....]
    ppermute x0 -> x7, waiting for transfers between devices: none -> 17.8 us  [on_device(): lax.ppermute(sent, 'row', [(i, i ^ turn) for i in range(size)])]
    unnamed x9 -> x16, local copies, waits for them, and re-layouts: 0.73 us -> 12.9 us
    ppermute x0 -> x7, starting transfers between devices: none -> 7.93 us  [on_device(): lax.ppermute(sent, 'row', [(i, i ^ turn) for i in range(size)])]
    all_to_all x1 -> x0, starting transfers between devices: 5.33 us -> none  [on_device(): lax.all_to_all(amp_tiles, 'row', split_axis=2, concat_axis=0, tiled=True)]
    gather x0 -> x1, local copies, waits for them, and re-layouts: none -> 5.31 us  [on_device(): blocks_2 = jnp.stack(finished)[here ^ jnp.arange(size)]]
    dot_general x1, matrix products: 22.3 us -> 17.9 us  [slot_products(): jnp.einsum('mrk,mkc->mrc', amp_slots, picked, preferred_element_type=jnp....]
  transfers between devices with their start and end apart: 2 -> 8, of which waited for: 2 -> 2; matrix products, arithmetic and copies ran while one was open for 7% -> 14% of each run, Pallas kernels for 0% -> 0%
where the time goes in v1:
time: 200 us; the launch traced here: 199 us
  waiting for transfers between devices  63.5 us (32%)
  other arithmetic  48 us (24%)
  local copies, waits for them, and re-layouts  37.4 us (19%)
  matrix products  17.9 us (9%)
  between operations  13.5 us (7%)
  blocking collectives  10.3 us (5%)
  starting transfers between devices  7.93 us (4%)
    reduce_scatter x1, waiting for transfers between devices, on_device(): lax.psum_scatter(row_terms(products, tile_ids, live_mask, lax.axis_size('...  45.7 us
    scatter-add x1, other arithmetic, row_terms(): jax.ops.segment_sum(products, target, num_segments=segment_total + 1)  45.1 us
    dot_general x1, matrix products, slot_products(): jnp.einsum('mrk,mkc->mrc', amp_slots, picked, preferred_element_type=jnp....  17.9 us
    ppermute x7, waiting for transfers between devices, on_device(): lax.ppermute(sent, 'row', [(i, i ^ turn) for i in range(size)])  17.8 us
    unnamed x16, local copies, waits for them, and re-layouts  12.9 us
    gather x1, local copies, waits for them, and re-layouts, slot_products(): picked = blocks[positions % blocks.shape[0]]  12.6 us
    all_to_all x1, blocking collectives, on_device(): lax.all_to_all(quotient, 'row', split_axis=0, concat_axis=0, tiled=True)  10.3 us
    ppermute x7, starting transfers between devices, on_device(): lax.ppermute(sent, 'row', [(i, i ^ turn) for i in range(size)])  7.93 us
  transfers between devices with their start and end apart: 8, of which 2 were waited for; matrix products, arithmetic and copies ran while one was open for 14% of the time, Pallas kernels for 0%

profile of v1, /device:TPU:0, one launch (start us, length us, event | category | flops | bytes accessed | tf_op | source)
XLA Modules:
  0.0 198.6 jit_solution(14194924993630660305)
XLA Ops:
  6.5 3.1 %constant_dynamic-slice_fusion = (bf16[1,1,1,16,128,128]{5,4,3,2,1,0:T(8,128)(2,1)S(1)}, bf16[1,1,1,16,128,128]{5,4,3,2,1,0:T(8,128)(2,1)S(1)}, bf16[1,1,1,16,12...) fusion(bf16[1,1,8,16,128,128]{5,4,3,2,1,0:T(8,128)(2,1)} %param, ...), kind=kLoop, calls=%fused_computation.21 | loop fusion | bytes 7340060 | tf_op jit(solution)/shard_map/dynamic_slice | solution.py:46
  9.7 0.5 collective-permute-start
  10.2 2.5 %collective-permute-start.1 = (bf16[1,1,1,16,128,128]{5,4,3,2,1,0:T(8,128)(2,1)S(1)}, bf16[1,1,1,16,128,128]{5,4,3,2,1,0:T(8,128)(2,1)}, u32[]{:S(2)}, u32[]{:S(2)}) collective-permute-start(bf16[1,1,1,16,128,128]{5,4,3,2,1,0:T(8,128)(2,1)S(1)} %get-tuple-element.11), channel_id=1, source_target_pairs={{0,8},{4,12},{8,0},{12,4},{16,24},{20,28},{24,16},{28,20},{1,9},{5... | collective-permute-start | bytes 1572872 | tf_op jit(solution)/shard_map/ppermute | solution.py:47
  12.7 0.1 collective-permute-start.2
  12.8 1.8 collective-permute-start.3
  14.6 0.8 remainder_reduce_fusion
  15.4 0.8 compare_reduce_fusion
  16.2 0.1 div.20
  16.3 0.3 dynamic-slice_reduce_fusion
  16.7 0.1 lt.98
  16.8 0.1 ne.52
  16.9 1.9 bitcast_dynamic-update-slice_fusion.7
  18.8 12.6 %gather_fusion.1 = bf16[128,128,512]{2,1,0:T(8,128)(2,1)} fusion(bf16[288,128,512]{2,1,0:T(8,128)(2,1)} %bitcast.32, s32[1024]{0:T(1024)S(1)} %pad_clamp_fusion), kind=kCustom, calls=%fused_computation.1 | custom fusion | bytes 33554944 | tf_op jit(solution)/shard_map/gather | solution.py:25
  31.4 2.1 %collective-permute-start.5 = (bf16[1,1,1,16,128,128]{5,4,3,2,1,0:T(8,128)(2,1)S(1)}, bf16[1,1,1,16,128,128]{5,4,3,2,1,0:T(8,128)(2,1)S(1)}, u32[]{:S(2)}, u32[]{:S(2)}) collective-permute-start(bf16[1,1,1,16,128,128]{5,4,3,2,1,0:T(8,128)(2,1)S(1)} %get-tuple-element.13), channel_id=1, source_target_pairs={{0,24},{4,28},{8,16},{12,20},{16,8},{20,12},{24,0},{28,4},{1,25},{... | collective-permute-start | bytes 1572872 | tf_op jit(solution)/shard_map/ppermute | solution.py:47
  33.4 1.9 bitcast_dynamic-update-slice_fusion.6
  35.3 1.0 collective-permute-start.6
  36.4 1.9 bitcast_dynamic-update-slice_fusion.5
  38.3 1.9 bitcast_dynamic-update-slice_fusion.4
  40.2 1.9 bitcast_dynamic-update-slice_fusion.3
  42.1 17.8 %collective-permute-done.4 = bf16[1,1,1,16,128,128]{5,4,3,2,1,0:T(8,128)(2,1)} collective-permute-done((bf16[1,1,1,16,128,128]{5,4,3,2,1,0:T(8,128)(2,1)S(1)}, bf16[1,1,1,16,128,128]{5,4,3,2,1,0:T(8,128)(2,1)}, u32[]{:S(2)}, u32[]{:S(2)}) %collective-permute-start.4) | collective-permute-done | bytes 524320 | tf_op jit(solution)/shard_map/ppermute | solution.py:47
  59.9 1.9 bitcast_dynamic-update-slice_fusion.2
  61.8 0.8 bitcast_dynamic-update-slice_fusion.1
  62.6 0.8 bitcast_dynamic-update-slice_fusion
  63.5 5.3 %gather_fusion = bf16[8,16,128,128]{3,2,1,0:T(8,128)(2,1)} fusion(bf16[8,16,128,128]{3,2,1,0:T(8,128)(2,1)} %bitcast.33, s32[1024]{0:T(1024)S(1)} %pad_clamp_fusion.1), kind=kCustom, calls=%fused_computation | custom fusion | bytes 8388640 | tf_op jit(solution)/shard_map/gather | solution.py:48
  68.8 17.9 %fusion.3 = f32[128,128,512]{2,1,0:T(8,128)} fusion(bf16[128,128,128]{2,1,0:T(8,128)(2,1)} %bitcast.30, bf16[128,128,512]{2,1,0:T(8,128)(2,1)} %gather_fusion.1), kind=kOutput, calls=%fused_computation.35 | convolution fusion | flops 2147483648 | bytes 54525952 | tf_op jit(solution)/shard_map/mrk,mkc->mrc/dot_general | solution.py:26
  86.7 0.3 broadcast_in_dim.3
  87.0 45.1 %scatter_fusion = f32[9,128,512]{2,1,0:T(8,128)S(1)} fusion(f32[9,128,512]{2,1,0:T(8,128)S(1)} %broadcast_in_dim.3, s32[128]{0:T(128)S(1)} %get-tuple-element.15, f32[128,128,512]{2,1,0:T(8,128)} %fusion.3), kind=kCustom, calls=%fused_computation.2 | custom fusion | flops 8388608 | bytes 100663808 | tf_op jit(solution)/shard_map/scatter-add | solution.py:34
  132.1 1.6 slice.8
  133.8 45.7 %reduce-scatter.2.cloned.1.call-done = f32[256,512]{1,0:T(8,128)} async-done(((f32[1024,512]{1,0:T(8,128)}), f32[256,512]{1,0:T(8,128)}) %reduce-scatter.2.cloned.1.call-update) | async-done | bytes 524304 | tf_op jit(solution)/shard_map/reduce_scatter | solution.py:56
  179.5 1.2 divide_convert_fusion
  180.7 10.3 %all_to_all.12 = bf16[8,32,512]{2,1,0:T(8,128)(2,1)S(1)} all-to-all(bf16[8,32,512]{2,1,0:T(8,128)(2,1)S(1)} %bitcast.34), channel_id=1, replica_groups=mesh['row'=8,'ck'=4] {'row'}, dimensions={0} | all-to-all | bytes 524288 | tf_op jit(solution)/shard_map/all_to_all | solution.py:63
  191.0 0.7 copy.16
  (23 shorter events, 0.3 us)
Async XLA Ops:
  6.5 9.8 %copy-start = (s32[8,1,8]{2,1,0:T(1,128)S(1)}, s32[8,1,8]{2,1,0:T(1,128)}, u32[]{:S(2)}) copy-start(s32[8,1,8]{2,1,0:T(1,128)} %param.8) | copy-start | bytes 772
  6.5 172.9 %reduce-scatter.2.cloned.1.call-start = ((), (), s32[]{:S(2)}) async-start(), calls=%async_computation.2 | async-start | bytes 2621440 | tf_op jit(solution)/shard_map/reduce_scatter | solution.py:56
  9.7 21.7 %collective-permute-start = (bf16[1,1,1,16,128,128]{5,4,3,2,1,0:T(8,128)(2,1)}, bf16[1,1,1,16,128,128]{5,4,3,2,1,0:T(8,128)(2,1)}, u32[]{:S(2)}, u32[]{:S(2)}) collective-permute-start(bf16[1,1,1,16,128,128]{5,4,3,2,1,0:T(8,128)(2,1)} %get-tuple-element.12), channel_id=1, source_target_pairs={{0,4},{4,0},{8,12},{12,8},{16,20},{20,16},{24,28},{28,24},{1,5},{5... | collective-permute-start | bytes 1572872 | tf_op jit(solution)/shard_map/ppermute | solution.py:47
  10.2 25.2 %collective-permute-start.1 = (bf16[1,1,1,16,128,128]{5,4,3,2,1,0:T(8,128)(2,1)S(1)}, bf16[1,1,1,16,128,128]{5,4,3,2,1,0:T(8,128)(2,1)}, u32[]{:S(2)}, u32[]{:S(2)}) collective-permute-start(bf16[1,1,1,16,128,128]{5,4,3,2,1,0:T(8,128)(2,1)S(1)} %get-tuple-element.11), channel_id=1, source_target_pairs={{0,8},{4,12},{8,0},{12,4},{16,24},{20,28},{24,16},{28,20},{1,9},{5... | collective-permute-start | bytes 1572872 | tf_op jit(solution)/shard_map/ppermute | solution.py:47
  12.7 25.6 %collective-permute-start.2 = (bf16[1,1,1,16,128,128]{5,4,3,2,1,0:T(8,128)(2,1)S(1)}, bf16[1,1,1,16,128,128]{5,4,3,2,1,0:T(8,128)(2,1)}, u32[]{:S(2)}, u32[]{:S(2)}) collective-permute-start(bf16[1,1,1,16,128,128]{5,4,3,2,1,0:T(8,128)(2,1)S(1)} %get-tuple-element.10), channel_id=1, source_target_pairs={{0,12},{4,8},{8,4},{12,0},{16,28},{20,24},{24,20},{28,16},{1,13},{... | collective-permute-start | bytes 1572872 | tf_op jit(solution)/shard_map/ppermute | solution.py:47
  12.8 27.4 %collective-permute-start.3 = (bf16[1,1,1,16,128,128]{5,4,3,2,1,0:T(8,128)(2,1)S(1)}, bf16[1,1,1,16,128,128]{5,4,3,2,1,0:T(8,128)(2,1)}, u32[]{:S(2)}, u32[]{:S(2)}) collective-permute-start(bf16[1,1,1,16,128,128]{5,4,3,2,1,0:T(8,128)(2,1)S(1)} %get-tuple-element.9), channel_id=1, source_target_pairs={{0,16},{4,20},{8,24},{12,28},{16,0},{20,4},{24,8},{28,12},{1,17},{... | collective-permute-start | bytes 1572872 | tf_op jit(solution)/shard_map/ppermute | solution.py:47
  14.5 45.3 %collective-permute-start.4 = (bf16[1,1,1,16,128,128]{5,4,3,2,1,0:T(8,128)(2,1)S(1)}, bf16[1,1,1,16,128,128]{5,4,3,2,1,0:T(8,128)(2,1)}, u32[]{:S(2)}, u32[]{:S(2)}) collective-permute-start(bf16[1,1,1,16,128,128]{5,4,3,2,1,0:T(8,128)(2,1)S(1)} %get-tuple-element.8), channel_id=1, source_target_pairs={{0,20},{4,16},{8,28},{12,24},{16,4},{20,0},{24,12},{28,8},{1,21},{... | collective-permute-start | bytes 1572872 | tf_op jit(solution)/shard_map/ppermute | solution.py:47
  31.4 30.4 %collective-permute-start.5 = (bf16[1,1,1,16,128,128]{5,4,3,2,1,0:T(8,128)(2,1)S(1)}, bf16[1,1,1,16,128,128]{5,4,3,2,1,0:T(8,128)(2,1)S(1)}, u32[]{:S(2)}, u32[]{:S(2)}) collective-permute-start(bf16[1,1,1,16,128,128]{5,4,3,2,1,0:T(8,128)(2,1)S(1)} %get-tuple-element.13), channel_id=1, source_target_pairs={{0,24},{4,28},{8,16},{12,20},{16,8},{20,12},{24,0},{28,4},{1,25},{... | collective-permute-start | bytes 1572872 | tf_op jit(solution)/shard_map/ppermute | solution.py:47
  35.3 27.3 %collective-permute-start.6 = (bf16[1,1,1,16,128,128]{5,4,3,2,1,0:T(8,128)(2,1)S(1)}, bf16[1,1,1,16,128,128]{5,4,3,2,1,0:T(8,128)(2,1)S(1)}, u32[]{:S(2)}, u32[]{:S(2)}) collective-permute-start(bf16[1,1,1,16,128,128]{5,4,3,2,1,0:T(8,128)(2,1)S(1)} %get-tuple-element.7), channel_id=1, source_target_pairs={{0,28},{4,24},{8,20},{12,16},{16,12},{20,8},{24,4},{28,0},{1,29},{... | collective-permute-start | bytes 1572872 | tf_op jit(solution)/shard_map/ppermute | solution.py:47
  87.0 104.7 %copy-start.1 = (s32[8,1,8]{2,1,0:T(1,128)S(1)}, s32[8,1,8]{2,1,0:T(1,128)}, u32[]{:S(2)}) copy-start(s32[8,1,8]{2,1,0:T(1,128)} %param.8) | copy-start | bytes 772
  132.1 47.4 %copy-start.2 = (f32[512]{0:T(512)S(1)}, f32[512]{0:T(512)}, u32[]{:S(2)}) copy-start(f32[512]{0:T(512)} %param.11) | copy-start | bytes 6148
  132.1 47.4 %copy-start.3 = (f32[256]{0:T(256)S(1)}, f32[256]{0:T(256)}, u32[]{:S(2)}) copy-start(f32[256]{0:T(256)} %param.10) | copy-start | bytes 3076
Sparse Core Ops, SparseCore 0:
  133.9 45.5 reduce-scatter.1
